TPU v7x, 32 devices: a whole 2x2x4 slice. The times are simulated.
32 devices in a mesh: pre: 4 (over x, core), dec: 8 (over z, y).
Axes of the slice: x: 2, y: 2, z: 4, core: 2. Of those that a mesh axis runs over, the one named last changes fastest.
Arguments:
- queries: bfloat16 [16, 128, 8192], P('pre', None, 'dec'), may hold values from -6 to 6, as said below
- branch_kv: bfloat16 [16, 128, 2048], P('pre', None, 'dec'), may hold values from -6 to 6
- pool_kv: bfloat16 [16, 128, 2048], P('pre', None, 'dec'), may hold values from -6 to 6, as said below
- page_lists: int32 [16, 16], replicated, may hold values from 0 to 15, as said below
- anc_len: int32 [16], replicated, may hold values from 1025 to 2048
- dec_owner: int32 [16], replicated, may hold values from 0 to 7, as said below
- output_projection_weight: bfloat16 [8192, 8192], P('dec'), may hold values from -0.0625 to 0.0625
Outputs:
- layer_out: bfloat16 [16, 128, 8192], P('pre', None, 'dec')
- decode_pages: bfloat16 [32, 128, 2048], P('dec', None, 'pre')
Inputs may be any that keep to these rules, and one draw needn't show every extreme that they name: `queries`: floats within the range. `pool_kv`: floats within the range. `page_lists`: each branch lists distinct pages; the first half of the slots holds the same pages for every branch. `dec_owner`: the 4 branches of one prefill device (branches p * 4 on) go to distinct decode owners; one decode owner receives a branch from every prefill device.
All inputs are finite; a program needn't handle non-finite values.
Results may differ from a plain program's by a relative error of at most 0.024.
Values may be sent and summed in bfloat16 or wider, within the bound.
A program may use at most 128 MiB of HBM per device.

v0:
```python
import functools
import math

import jax
import jax.numpy as jnp
from jax import lax
from jax.experimental import pallas as pl
from jax.experimental.pallas import tpu as pltpu
from jax.sharding import PartitionSpec as P

HD = 128
MASKED = -1e30
SCALE = HD**-0.5 * math.log2(math.e)
MESH = pl.DeviceIdType.MESH
VMEM = pl.BlockSpec(memory_space=pltpu.VMEM)


def from_partner(value, axis, stride):
    mask = 2**stride
    pairs = [(source, source ^ mask) for source in range(lax.axis_size(axis))]
    return lax.ppermute(value, axis, pairs)


def visibility_bias(lists, counts, page_count, page_len):
    slots = lists.shape[1]
    page_ids = jnp.arange(page_count, dtype=jnp.int32)
    reach = jnp.clip(
        counts[:, None] - jnp.arange(slots, dtype=jnp.int32)[None, :] * page_len, 0, page_len
    )
    match = lists[:, :, None] == page_ids[None, None, :]
    visible_count = jnp.sum(jnp.where(match, reach[:, :, None], 0), axis=1)
    tokens = jnp.arange(page_len, dtype=jnp.int32)
    allowed = tokens[None, None, :] < visible_count[:, :, None]
    allowed = allowed.reshape(lists.shape[0], 1, page_count * page_len)
    return jnp.where(allowed, 0.0, MASKED).astype(jnp.float32)


def load_values(pool_ref, values):
    pages, page_len, _ = pool_ref.shape
    values[:, :HD] = pool_ref[:, :, HD:].reshape(pages * page_len, HD)
    values[:, HD:] = jnp.ones((pages * page_len, HD), values.dtype)


def attend(branch, q_ref, own_ref, pool_ref, bias_ref, values, result_ref):
    pages, page_len, _ = pool_ref.shape
    heads = q_ref.shape[2] // HD
    pair = 2
    keys = pool_ref[:, :, :HD].reshape(pages * page_len, HD)
    own_keys = own_ref[branch, :, :HD]
    own_values = own_ref[branch, :, HD:]
    own_values = jnp.concatenate([own_values, jnp.ones_like(own_values)], 1)
    row = lax.broadcasted_iota(jnp.int32, (page_len, page_len), 0)
    col = lax.broadcasted_iota(jnp.int32, (page_len, page_len), 1)
    causal = jnp.where(col <= row, 0.0, MASKED)
    causal = jnp.concatenate([causal] * pair, 0)
    bias = bias_ref[branch]
    nt = (((1,), (1,)), ((), ()))

    def group(g, carry):
        start = pl.multiple_of(g * pair * HD, pair * HD)
        q = q_ref[branch, :, pl.ds(start, pair * HD)]
        q = jnp.concatenate([q[:, i * HD : (i + 1) * HD] for i in range(pair)], 0)
        far = lax.dot_general(q, keys, nt, preferred_element_type=jnp.float32) + bias
        near = lax.dot_general(q, own_keys, nt, preferred_element_type=jnp.float32) + causal
        top = jnp.maximum(
            jnp.max(far, axis=-1, keepdims=True), jnp.max(near, axis=-1, keepdims=True)
        )
        top = top * SCALE
        far = jnp.exp2(far * SCALE - top).astype(jnp.bfloat16)
        near = jnp.exp2(near * SCALE - top).astype(jnp.bfloat16)
        out = jnp.dot(far, values[...], preferred_element_type=jnp.float32)
        out = out + jnp.dot(near, own_values, preferred_element_type=jnp.float32)
        out = (out[:, :HD] / out[:, HD:]).astype(jnp.bfloat16)
        for i in range(pair):
            result_ref[branch, :, pl.ds(start + i * HD, HD)] = out[
                i * page_len : (i + 1) * page_len
            ]
        return carry

    lax.fori_loop(0, heads // pair, group, 0)


def bits_of(index, count):
    return [lax.rem(index // 2**k, 2) for k in range(count)]


def flipped(bits, rel):
    total = 0
    for k, bit in enumerate(bits):
        total = total + 2**k * (1 - bit if rel // 2**k % 2 else bit)
    return total


def halving(order):
    stages = []
    for s, bit in enumerate(order):
        done = [2**k for k in order[:s]]
        rest = [2**k for k in order[s + 1 :]]
        rels = [2**bit]
        for mask in reversed(rest):
            rels = [r + mask for r in rels] + rels
        stages.append([(r, bit, [r + m for m in done]) for r in rels])
    stages.append([(0, None, [2**k for k in order])])
    return stages


def layer_kernel(
    n_pre,
    n_dec,
    cuts,
    pool_ref,
    bucket_ref,
    q_hbm,
    own_hbm,
    bias_ref,
    w_ref,
    out_ref,
    pages_ref,
    all_ref,
    q_ref,
    own_ref,
    values,
    attn,
    wv,
    sent,
    got,
    load_sem,
    wsem,
    psend,
    precv,
    bsend,
    brecv,
    ssem,
    rsem,
):
    pre = lax.axis_index("pre")
    dec = lax.axis_index("dec")
    branches, page_len, cols = out_ref.shape
    count = pool_ref.shape[0]
    width = bucket_ref.shape[2]
    ratio = n_dec // n_pre
    chips = n_pre // 2
    chip = pre // 2
    core = lax.rem(pre, 2)
    log = n_dec.bit_length() - 1
    bits = bits_of(dec, log)

    def block_of(device):
        return pl.ds(device * count, count)

    def across(k):
        return pltpu.make_async_remote_copy(
            src_ref=pool_ref,
            dst_ref=all_ref.at[block_of(pre)],
            send_sem=psend.at[k],
            recv_sem=precv.at[k],
            device_id={"pre": lax.rem(chip + k, chips) * 2 + core},
            device_id_type=MESH,
        )

    def beside(k):
        where = all_ref.at[block_of(lax.rem(chip + chips - k, chips) * 2 + core)]
        return pltpu.make_async_remote_copy(
            src_ref=pool_ref if k == 0 else where,
            dst_ref=where,
            send_sem=psend.at[chips + k],
            recv_sem=precv.at[chips + k],
            device_id={"pre": chip * 2 + 1 - core},
            device_id_type=MESH,
        )

    for k in range(1, chips):
        across(k).start()
    beside(0).start()
    loads = [
        pltpu.make_async_copy(pool_ref, all_ref.at[block_of(pre)], load_sem.at[0]),
        pltpu.make_async_copy(q_hbm, q_ref, load_sem.at[1]),
        pltpu.make_async_copy(own_hbm, own_ref, load_sem.at[2]),
    ]
    for copy in loads:
        copy.start()

    def load(rel):
        start = pl.multiple_of(flipped(bits, rel) * cols, cols)
        return pltpu.make_async_copy(w_ref.at[:, pl.ds(start, cols)], wv.at[rel], wsem.at[rel])

    for rel in range(n_dec):
        load(rel).start()

    home = dec // ratio
    part = lax.rem(dec, ratio)
    column = pl.multiple_of(part * width, 128)

    def bucket_copy(k):
        owner = lax.rem(dec + k, n_dec)
        return pltpu.make_async_remote_copy(
            src_ref=bucket_ref.at[owner],
            dst_ref=pages_ref.at[pre, :, pl.ds(column, width)],
            send_sem=bsend.at[k],
            recv_sem=brecv.at[pre, part],
            device_id={"pre": home, "dec": owner},
            device_id_type=MESH,
        )

    for k in range(1, chips):
        across(k).wait_recv()
        beside(k).start()

    for k in range(1, n_dec):
        bucket_copy(k).start()

    @pl.when(home == pre)
    def _():
        pltpu.make_async_copy(
            bucket_ref.at[dec], pages_ref.at[pre, :, pl.ds(column, width)], brecv.at[pre, part]
        ).start()

    @pl.when(home != pre)
    def _():
        bucket_copy(0).start()

    for copy in loads:
        copy.wait()
    for k in range(chips):
        beside(k).wait_recv()
    load_values(all_ref, values)

    def piece(ref, rel, b, cut):
        return ref.at[rel, b, :, pl.ds(cuts[cut][0], cuts[cut][1])]

    def term_copy(rel, bit, b, cut):
        return pltpu.make_async_remote_copy(
            src_ref=piece(sent, rel, b, cut),
            dst_ref=piece(got, rel, b, cut),
            send_sem=ssem.at[cut, rel, b],
            recv_sem=rsem.at[cut, rel, b],
            device_id={"dec": flipped(bits, 2**bit)},
            device_id_type=MESH,
        )

    plans = [halving(order) for _, _, order in cuts]

    def senders(cut):
        return [(rel, bit) for stage in plans[cut][:-1] for rel, bit, _ in stage]

    bit_of = [dict(senders(cut)) for cut in range(len(cuts))]

    def run_stage(stage, b):
        for cut, (begin, size, _) in enumerate(cuts):
            for rel, bit, parts in plans[cut][stage]:
                for other in parts:
                    term_copy(other, bit_of[cut][other], b, cut).wait_recv()
                step = math.gcd(size, 512)

                def tile(i, carry, rel=rel, begin=begin, parts=parts, step=step, bit=bit):
                    at = pl.ds(pl.multiple_of(begin + i * step, step), step)
                    total = jnp.dot(
                        attn[b], wv[rel, :, at], preferred_element_type=jnp.float32
                    )
                    for other in parts:
                        total = total + got[other, b, :, at].astype(jnp.float32)
                    if bit is None:
                        out_ref[b, :, at] = total.astype(jnp.bfloat16)
                    else:
                        sent[rel, b, :, at] = total.astype(jnp.bfloat16)
                    return carry

                lax.fori_loop(0, size // step, tile, 0)
                if bit is not None:
                    term_copy(rel, bit, b, cut).start()

    def turn(i, carry):
        @pl.when(i < branches)
        def _():
            attend(i, q_ref, own_ref, all_ref, bias_ref, values, attn)

        @pl.when(i == 0)
        def _():
            for rel in range(n_dec):
                load(rel).wait()

        for stage in range(log + 1):
            @pl.when(jnp.logical_and(i >= stage, i < branches + stage))
            def _(stage=stage):
                run_stage(stage, i - stage)

        return carry

    lax.fori_loop(0, branches + log, turn, 0)

    def drain(b, carry):
        for cut in range(len(cuts)):
            for rel, bit in senders(cut):
                term_copy(rel, bit, b, cut).wait_send()
        return carry

    lax.fori_loop(0, branches, drain, 0)
    for k in range(1, chips):
        across(k).wait_send()
    for k in range(chips):
        beside(k).wait_send()
    for k in range(1, n_dec):
        bucket_copy(k).wait_send()

    @pl.when(home != pre)
    def _():
        bucket_copy(0).wait_send()

    for source in range(n_pre):
        for spot in range(ratio):
            where = pages_ref.at[source, :, pl.ds(spot * width, width)]
            pltpu.make_async_copy(where, where, brecv.at[source, spot]).wait()


def layer(pool, buckets, queries, own, bias, weight, n_pre, n_dec):
    branches, page_len, depth = queries.shape
    count = pool.shape[0]
    cols = weight.shape[1] // n_dec
    ratio = n_dec // n_pre
    log = n_dec.bit_length() - 1
    straight = tuple(range(log))
    other = (1, 0) + straight[2:]
    part = cols // 2
    cuts = ((0, part, other), (part, cols - part, straight))
    bf16 = jnp.bfloat16
    anywhere = pl.BlockSpec(memory_space=pl.ANY)
    return pl.pallas_call(
        functools.partial(layer_kernel, n_pre, n_dec, cuts),
        out_shape=(
            jax.ShapeDtypeStruct((branches, page_len, cols), bf16),
            jax.ShapeDtypeStruct((n_pre, page_len, ratio * buckets.shape[2]), bf16),
        ),
        in_specs=[anywhere] * 4 + [VMEM, anywhere],
        out_specs=(VMEM, VMEM),
        scratch_shapes=[
            pltpu.VMEM((count * n_pre,) + pool.shape[1:], bf16),
            pltpu.VMEM(queries.shape, bf16),
            pltpu.VMEM(own.shape, bf16),
            pltpu.VMEM((count * n_pre * page_len, 2 * HD), bf16),
            pltpu.VMEM(queries.shape, bf16),
            pltpu.VMEM((n_dec, depth, cols), bf16),
            pltpu.VMEM((n_dec, branches, page_len, cols), bf16),
            pltpu.VMEM((n_dec, branches, page_len, cols), bf16),
            pltpu.SemaphoreType.DMA((3,)),
            pltpu.SemaphoreType.DMA((n_dec,)),
            pltpu.SemaphoreType.DMA((n_pre,)),
            pltpu.SemaphoreType.DMA((n_pre,)),
            pltpu.SemaphoreType.DMA((n_dec,)),
            pltpu.SemaphoreType.DMA((n_pre, ratio)),
            pltpu.SemaphoreType.DMA((2, n_dec, branches)),
            pltpu.SemaphoreType.DMA((2, n_dec, branches)),
        ],
        compiler_params=pltpu.CompilerParams(
            has_side_effects=True, vmem_limit_bytes=62 * 2**20
        ),
        name="layer",
    )(pool, buckets, queries, own, bias, weight)


def on_device(
    queries, branch_kv, pool_kv, page_lists, anc_len, dec_owner, output_projection_weight
):
    n_pre = lax.axis_size("pre")
    n_dec = lax.axis_size("dec")
    pre_idx = lax.axis_index("pre")
    dec_idx = lax.axis_index("dec")
    branch_count, page_len, _ = queries.shape
    kv_cols = pool_kv.shape[2]
    if kv_cols < 2 * HD:
        other_pool, other_own = from_partner((pool_kv, branch_kv), "dec", 0)
        first_half = dec_idx % 2 == 0
        pool = jnp.where(
            first_half,
            jnp.concatenate([pool_kv, other_pool], 2),
            jnp.concatenate([other_pool, pool_kv], 2),
        )
        own = jnp.where(
            first_half,
            jnp.concatenate([branch_kv, other_own], 2),
            jnp.concatenate([other_own, branch_kv], 2),
        )
    else:
        pool, own = pool_kv, branch_kv

    start = pre_idx * branch_count
    my_lists = lax.dynamic_slice_in_dim(page_lists, start, branch_count, 0)
    my_counts = lax.dynamic_slice_in_dim(anc_len, start, branch_count, 0)
    owners = lax.dynamic_slice_in_dim(dec_owner, start, branch_count, 0)
    onehot = owners[:, None] == jnp.arange(n_dec, dtype=jnp.int32)[None, :]
    buckets = jnp.zeros((n_dec,) + branch_kv.shape[1:], branch_kv.dtype)
    for b in range(branch_count):
        buckets = jnp.where(onehot[b][:, None, None], branch_kv[b][None], buckets)

    bias = visibility_bias(my_lists, my_counts, pool.shape[0] * n_pre, page_len)
    layer_out, decode_pages = layer(
        pool, buckets, queries, own, bias, output_projection_weight, n_pre, n_dec
    )
    return (layer_out, decode_pages)


def solution(mesh):
    in_specs = (
        P("pre", None, "dec"),
        P("pre", None, "dec"),
        P("pre", None, "dec"),
        P(),
        P(),
        P(),
        P("dec", None),
    )
    out_specs = (P("pre", None, "dec"), P("dec", None, "pre"))
    return jax.shard_map(
        on_device, mesh=mesh, in_specs=in_specs, out_specs=out_specs, check_vma=False
    )
```

profile of v0, /device:TPU:0, one launch (start us, length us, event | category | flops | bytes accessed | tf_op | source)
XLA Modules:
  0.0 133.7 jit_solution(11036966867719568794)
XLA Ops:
  0.6 0.7 dynamic_slice.11
  1.4 0.7 dynamic_slice.9
  2.1 0.1 iota_compare_fusion.1
  2.2 0.8 subtract_clamp_fusion
  3.0 0.1 select_reduce_fusion
  3.1 0.1 lt.36
  3.1 0.7 compare_select_fusion.bias_ref
  3.8 1.0 slice_bitcast_fusion.3
  4.7 1.1 select_select_fusion.bucket_ref
  5.8 123.7 %layer.1 = (bf16[4,128,1024]{2,1,0:T(8,128)(2,1)}, bf16[4,128,512]{2,1,0:T(8,128)(2,1)}) custom-call(bf16[4,128,256]{2,1,0:T(8,128)(2,1)} %pool_ref.1, bf16[8,128,256]{2,1,0:T(8,128)(2,1)} %select_select_fusion.bucket_ref, bf16[4,128,1024]{2,1,0:T(8,128)(2,1)} %q_hbm.1, bf16[4,128,256]{2,1,0:T(8,128)(2,1)} %own_hbm.1, ...), custom_call_target="tpu_custom_call" | custom-call | tf_op jit(solution)/shard_map/layer/pallas_call | solution.py:327
  129.5 2.3 %copy.11 = bf16[4,128,1024]{2,1,0:T(8,128)(2,1)} copy(bf16[4,128,1024]{2,1,0:T(8,128)(2,1)} %get-tuple-element.14) | data formatting | bytes 2097152
  131.8 1.9 %copy.12 = bf16[4,128,512]{2,1,0:T(8,128)(2,1)} copy(bf16[4,128,512]{2,1,0:T(8,128)(2,1)} %get-tuple-element.15) | data formatting | bytes 1048576
  (3 shorter events, 0.0 us)
where the time goes:
time: 134 us
  Pallas kernels  124 us (93%)
  local copies, waits for them, and re-layouts  6.62 us (5%)
  other arithmetic  2.64 us (2%)
    pallas_call x1, Pallas kernels, layer(): pl.pallas_call(functools.partial(layer_kernel, n_pre, n_dec, cuts), out_s...  124 us
    unnamed x2, local copies, waits for them, and re-layouts  4.13 us

commit v1 on v0

v1 whole, which is shorter than its diff:
```python
import functools
import math

import jax
import jax.numpy as jnp
from jax import lax
from jax.experimental import pallas as pl
from jax.experimental.pallas import tpu as pltpu
from jax.sharding import PartitionSpec as P

HD = 128
MASKED = -1e30
SCALE = HD**-0.5 * math.log2(math.e)
MESH = pl.DeviceIdType.MESH
VMEM = pl.BlockSpec(memory_space=pltpu.VMEM)
SMEM = pl.BlockSpec(memory_space=pltpu.SMEM)
PAIR = 2
WPIECES = 4
CHUNKS = 2


def from_partner(value, axis, stride):
    mask = 2**stride
    pairs = [(source, source ^ mask) for source in range(lax.axis_size(axis))]
    return lax.ppermute(value, axis, pairs)


def load_values(pool_ref, values):
    pages, page_len, _ = pool_ref.shape
    values[:, :HD] = pool_ref[:, :, HD:].reshape(pages * page_len, HD)
    values[:, HD:] = jnp.ones((pages * page_len, HD), values.dtype)


def attend(branch, first, last, q_ref, own_ref, pool_ref, bias_ref, values, attn, after):
    pages, page_len, _ = pool_ref.shape
    keys = pool_ref[:, :, :HD].reshape(pages * page_len, HD)
    own_keys = own_ref[branch, :, :HD]
    own_values = own_ref[branch, :, HD:]
    own_values = jnp.concatenate([own_values, jnp.ones_like(own_values)], 1)
    row = lax.broadcasted_iota(jnp.int32, (page_len, page_len), 0)
    col = lax.broadcasted_iota(jnp.int32, (page_len, page_len), 1)
    causal = jnp.where(col <= row, 0.0, MASKED)
    causal = jnp.concatenate([causal] * PAIR, 0)
    bias = bias_ref[branch]
    nt = (((1,), (1,)), ((), ()))

    def group(g, carry):
        start = pl.multiple_of(g * PAIR * HD, PAIR * HD)
        q = q_ref[branch, :, pl.ds(start, PAIR * HD)]
        q = jnp.concatenate([q[:, i * HD : (i + 1) * HD] for i in range(PAIR)], 0)
        far = lax.dot_general(q, keys, nt, preferred_element_type=jnp.float32) + bias
        near = lax.dot_general(q, own_keys, nt, preferred_element_type=jnp.float32) + causal
        top = jnp.maximum(
            jnp.max(far, axis=-1, keepdims=True), jnp.max(near, axis=-1, keepdims=True)
        )
        top = top * SCALE
        far = jnp.exp2(far * SCALE - top).astype(jnp.bfloat16)
        near = jnp.exp2(near * SCALE - top).astype(jnp.bfloat16)
        out = jnp.dot(far, values[...], preferred_element_type=jnp.float32)
        out = out + jnp.dot(near, own_values, preferred_element_type=jnp.float32)
        out = (out[:, :HD] / out[:, HD:]).astype(jnp.bfloat16)
        for i in range(PAIR):
            attn[branch, :, pl.ds(start + i * HD, HD)] = out[i * page_len : (i + 1) * page_len]
        after(branch, g)
        return carry

    lax.fori_loop(first, last, group, 0)


def layer_kernel(
    n_pre,
    n_dec,
    lists_ref,
    reach_ref,
    owner_ref,
    kv_ref,
    pool_ref,
    q_hbm,
    own_hbm,
    w_ref,
    out_ref,
    pages_ref,
    all_ref,
    q_ref,
    own_ref,
    values,
    attn,
    wv,
    sent,
    got,
    bias_ref,
    bucket_ref,
    row_ref,
    block_ref,
    load_sem,
    wsem,
    psend,
    precv,
    bsend,
    brecv,
    msend,
    mrecv,
    hsend,
    hrecv,
    asend,
    arecv,
    ysend,
    yrecv,
    xsend,
    xrecv,
    csend,
    crecv,
    ssem,
    rsem,
):
    pre = lax.axis_index("pre")
    dec = lax.axis_index("dec")
    branches, page_len, cols = out_ref.shape
    depth = w_ref.shape[0]
    count = pool_ref.shape[0]
    width = kv_ref.shape[2]
    ratio = n_dec // n_pre
    chips = n_pre // 2
    chip = pre // 2
    core = lax.rem(pre, 2)
    spots = n_dec // 2
    spot = dec // 2
    side = lax.rem(dec, 2)
    mate = dec + 1 - 2 * side
    share = depth // n_pre
    pieces = WPIECES
    piece = cols // pieces
    halves = CHUNKS
    half = cols // halves
    per_half = pieces // halves
    groups = depth // (PAIR * HD)
    low = 2 * spot < spots

    def target(step):
        outer = spots - 1 - spot
        rising = jnp.where(step < outer, spots - 1 - step, step - outer)
        falling = jnp.where(step < spot, step, spots - 1 - step + spot)
        return jnp.where(low, rising, falling)

    def block_of(device):
        return pl.ds(device * count, count)

    def across(k):
        return pltpu.make_async_remote_copy(
            src_ref=pool_ref,
            dst_ref=all_ref.at[block_of(pre)],
            send_sem=psend.at[k],
            recv_sem=precv.at[k],
            device_id={"pre": lax.rem(chip + k, chips) * 2 + core},
            device_id_type=MESH,
        )

    def beside(k):
        where = all_ref.at[block_of(lax.rem(chip + chips - k, chips) * 2 + core)]
        return pltpu.make_async_remote_copy(
            src_ref=pool_ref if k == 0 else where,
            dst_ref=where,
            send_sem=psend.at[chips + k],
            recv_sem=precv.at[chips + k],
            device_id={"pre": chip * 2 + 1 - core},
            device_id_type=MESH,
        )

    def own_rows(step):
        t = target(step)
        start = pl.multiple_of((2 * t + side) * cols, cols)
        return pltpu.make_async_copy(
            w_ref.at[:, pl.ds(start, cols)], wv.at[t, pl.ds(0, depth)], wsem.at[step]
        )

    def share_of(device, step, c):
        rows = pl.ds(pl.multiple_of(depth + device * share, 16), share)
        return wv.at[target(step), rows, pl.ds(pl.multiple_of(c * piece, piece), piece)]

    def to_mate(step, c):
        start = pl.multiple_of((2 * target(step) + 1 - side) * cols + c * piece, piece)
        rows = pl.ds(pl.multiple_of(pre * share, 16), share)
        return pltpu.make_async_remote_copy(
            src_ref=w_ref.at[rows, pl.ds(start, piece)],
            dst_ref=share_of(pre, step, c),
            send_sem=ysend.at[step, c],
            recv_sem=yrecv.at[step, c],
            device_id={"dec": mate},
            device_id_type=MESH,
        )

    def to_chip(step, c, k):
        return pltpu.make_async_remote_copy(
            src_ref=share_of(pre, step, c),
            dst_ref=share_of(pre, step, c),
            send_sem=xsend.at[step, c, k],
            recv_sem=xrecv.at[step, c, k],
            device_id={"pre": lax.rem(chip + k, chips) * 2 + core},
            device_id_type=MESH,
        )

    def to_core(step, c, k):
        where = share_of(lax.rem(chip + chips - k, chips) * 2 + core, step, c)
        return pltpu.make_async_remote_copy(
            src_ref=where,
            dst_ref=where,
            send_sem=csend.at[step, c, k],
            recv_sem=crecv.at[step, c, k],
            device_id={"pre": chip * 2 + 1 - core},
            device_id_type=MESH,
        )

    def pass_on(step, c):
        to_mate(step, c).wait_recv()
        for k in range(1, chips):
            to_chip(step, c, k).start()
        to_core(step, c, 0).start()

    def pass_over(step, c):
        for k in range(1, chips):
            to_chip(step, c, k).wait_recv()
            to_core(step, c, k).start()

    def need(step, c):
        for k in range(chips):
            to_core(step, c, k).wait_recv()

    def attn_copy(b, g):
        start = pl.multiple_of(g * PAIR * HD, PAIR * HD)
        return pltpu.make_async_remote_copy(
            src_ref=attn.at[b, :, pl.ds(start, PAIR * HD)],
            dst_ref=attn.at[b, :, pl.ds(depth + start, PAIR * HD)],
            send_sem=asend.at[b, g],
            recv_sem=arecv.at[b, g],
            device_id={"dec": mate},
            device_id_type=MESH,
        )

    def at_half(c):
        return pl.ds(pl.multiple_of(c * half, half), half)

    def arrival(slot, b, c):
        where = got.at[slot, b, :, at_half(c)]
        return pltpu.make_async_copy(where, where, rsem.at[slot, b, c])

    def chunk_copy(step, b, c):
        t = target(step)
        onward = t > spot
        slot = jnp.where(t == spot - 1, spots, t)
        return pltpu.make_async_remote_copy(
            src_ref=sent.at[t, b, :, at_half(c)],
            dst_ref=got.at[slot, b, :, at_half(c)],
            send_sem=ssem.at[step, b, c],
            recv_sem=rsem.at[slot, b, c],
            device_id={"dec": jnp.where(onward, dec + 2, dec - 2)},
            device_id_type=MESH,
        )

    def send_chunk(step, b, c):
        t = target(step)
        relayed = jnp.where(t > spot, spot > 0, spot < spots - 1)

        @pl.when(relayed)
        def _():
            arrival(t, b, c).wait()

        total = jnp.dot(attn[b], wv[t, :, at_half(c)], preferred_element_type=jnp.float32)
        total = total + got[t, b, :, at_half(c)].astype(jnp.float32)
        sent[t, b, :, at_half(c)] = total.astype(jnp.bfloat16)
        chunk_copy(step, b, c).start()

    def last_chunk(b, c):
        @pl.when(spot > 0)
        def _():
            arrival(spot, b, c).wait()

        @pl.when(spot < spots - 1)
        def _():
            arrival(spots, b, c).wait()

        total = jnp.dot(attn[b], wv[spot, :, at_half(c)], preferred_element_type=jnp.float32)
        total = total + got[spot, b, :, at_half(c)].astype(jnp.float32)
        total = total + got[spots, b, :, at_half(c)].astype(jnp.float32)
        out_ref[b, :, at_half(c)] = total.astype(jnp.bfloat16)

    def to_row(k):
        where = lax.rem(spot + k, spots)
        return pltpu.make_async_remote_copy(
            src_ref=bucket_ref.at[where],
            dst_ref=row_ref.at[spot],
            send_sem=bsend.at[k],
            recv_sem=brecv.at[k],
            device_id={"dec": 2 * where + side},
            device_id_type=MESH,
        )

    row_local = pltpu.make_async_copy(bucket_ref.at[spot], row_ref.at[spot], brecv.at[0])
    to_side = pltpu.make_async_remote_copy(
        src_ref=row_ref.at[:, 1 - side],
        dst_ref=block_ref.at[side],
        send_sem=msend.at[0],
        recv_sem=mrecv.at[0],
        device_id={"dec": mate},
        device_id_type=MESH,
    )
    side_local = pltpu.make_async_copy(row_ref.at[:, side], block_ref.at[side], mrecv.at[1])

    def home_parts(k, part):
        home = lax.rem(pre + k, n_pre)
        source = home * ratio + part
        src = block_ref.at[lax.rem(source, 2), source // 2]
        return home, src, pages_ref.at[pre, :, pl.ds(part * width, width)]

    def to_home(k, part):
        home, src, dst = home_parts(k, part)
        return pltpu.make_async_remote_copy(
            src_ref=src,
            dst_ref=dst,
            send_sem=hsend.at[k, part],
            recv_sem=hrecv.at[k, part],
            device_id={"pre": home},
            device_id_type=MESH,
        )

    def home_local(part):
        _, src, dst = home_parts(0, part)
        return pltpu.make_async_copy(src, dst, hrecv.at[0, part])

    def pages_to_side():
        for k in range(1, spots):
            to_row(k).wait_recv()
        row_local.wait()
        to_side.start()
        side_local.start()

    def pages_to_home():
        to_side.wait_recv()
        side_local.wait()
        for part in range(ratio):
            home_local(part).start()
            for k in range(1, n_pre):
                to_home(k, part).start()

    barrier = pltpu.get_barrier_semaphore()
    for k in range(1, n_pre):
        pl.semaphore_signal(
            barrier, 1, device_id={"pre": lax.rem(pre + k, n_pre)}, device_id_type=MESH
        )
    pl.semaphore_signal(barrier, 1, device_id={"dec": mate}, device_id_type=MESH)
    for k in range(1, spots):
        pl.semaphore_signal(
            barrier,
            1,
            device_id={"dec": 2 * lax.rem(spot + k, spots) + side},
            device_id_type=MESH,
        )
    loads = [
        pltpu.make_async_copy(pool_ref, all_ref.at[block_of(pre)], load_sem.at[0]),
        pltpu.make_async_copy(q_hbm, q_ref, load_sem.at[1]),
        pltpu.make_async_copy(own_hbm, own_ref, load_sem.at[2]),
    ]
    for copy in loads:
        copy.start()
    own_rows(0).start()
    pl.semaphore_wait(barrier, n_pre + spots - 1)

    for k in range(1, chips):
        across(k).start()
    beside(0).start()
    for c in range(pieces):
        to_mate(0, c).start()
    first = pre * branches
    for o in range(n_dec):
        bucket = jnp.zeros(kv_ref.shape[1:], kv_ref.dtype)
        for b in range(branches):
            bucket = jnp.where(owner_ref[first + b] == o, kv_ref[b], bucket)
        bucket_ref[o // 2, o % 2] = bucket
    for k in range(1, spots):
        to_row(k).start()
    row_local.start()

    def mask(b, carry):
        visible = jnp.zeros((count * n_pre, page_len), jnp.int32)
        page = lax.broadcasted_iota(jnp.int32, visible.shape, 0)
        token = lax.broadcasted_iota(jnp.int32, visible.shape, 1)
        for slot in range(lists_ref.shape[1]):
            shown = reach_ref[first + b] - slot * page_len
            visible = jnp.where(page == lists_ref[first + b, slot], shown, visible)
        bias = jnp.where(token < visible, 0.0, MASKED).astype(jnp.float32)
        for p in range(count * n_pre):
            bias_ref[b, :, p * page_len : (p + 1) * page_len] = bias[p : p + 1]
        return carry

    lax.fori_loop(0, branches, mask, 0)

    @pl.when(spot == 0)
    def _():
        def clear(t, carry):
            got[t] = jnp.zeros(got.shape[1:], got.dtype)
            return carry

        lax.fori_loop(0, spots, clear, 0)

    @pl.when(spot == spots - 1)
    def _():
        def clear(t, carry):
            got[t + t // (spots - 1)] = jnp.zeros(got.shape[1:], got.dtype)
            return carry

        lax.fori_loop(0, spots, clear, 0)

    for k in range(1, chips):
        across(k).wait_recv()
        beside(k).start()

    for c in range(pieces // 2):
        pass_on(0, c)
    for copy in loads:
        copy.wait()
    for k in range(chips):
        beside(k).wait_recv()
    load_values(all_ref, values)

    def load_rest(step, carry):
        own_rows(step).start()
        return carry

    lax.fori_loop(1, spots, load_rest, 0)

    def after(b, g):
        attn_copy(b, g).start()

    def some(i, first, last):
        @pl.when(i < branches)
        def _():
            attend(
                i, first, last, q_ref, own_ref, all_ref, bias_ref, values, attn, after
            )

    def turn(i, carry):
        some(i, 0, groups // 2)

        @pl.when(i == 0)
        def _():
            for c in range(pieces // 2, pieces):
                pass_on(0, c)
            for c in range(pieces // 2):
                pass_over(0, c)

        @pl.when(i > 0)
        def _():
            b = i - 1

            @pl.when(i == 1)
            def _():
                own_rows(0).wait()

            for g in range(groups):
                attn_copy(b, g).wait_recv()
            for c in range(halves):
                @pl.when(i == 1)
                def _(c=c):
                    for p in range(c * per_half, (c + 1) * per_half):
                        need(0, p)

                send_chunk(0, b, c)

        some(i, groups // 2, groups)

        @pl.when(i == 0)
        def _():
            for c in range(pieces // 2, pieces):
                pass_over(0, c)

        @pl.when(i == 0)
        def _():
            to_mate(1, 0).start()

        @pl.when(i == 2)
        def _():
            to_mate(1, 1).start()
            pages_to_side()

        @pl.when(i == branches - 1)
        def _():
            for c in range(2, pieces):
                to_mate(1, c).start()
            if spots > 2:
                for c in range(pieces):
                    to_mate(2, c).start()
            for c in range(per_half):
                pass_on(1, c)

        @pl.when(i == branches)
        def _():
            pages_to_home()
            for c in range(per_half):
                pass_over(1, c)
            for c in range(per_half, pieces):
                pass_on(1, c)

        return carry

    lax.fori_loop(0, branches + 1, turn, 0)

    def ahead(act, step, c, by):
        later = c + by
        where = step + later // halves
        first = later % halves * per_half

        @pl.when(where < spots)
        def _():
            for p in range(first, first + per_half):
                act(where, p)

    def phase(step, carry):
        own_rows(step).wait()

        @pl.when(step + 2 < spots)
        def _():
            for p in range(pieces):
                to_mate(step + 2, p).start()

        for c in range(halves):
            for p in range(c * per_half, (c + 1) * per_half):
                need(step, p)

            def over(b, inner, c=c):
                @pl.when(step < spots - 1)
                def _():
                    send_chunk(step, b, c)

                @pl.when(step == spots - 1)
                def _():
                    last_chunk(b, c)

                return inner

            lax.fori_loop(0, branches // 2, over, 0)
            ahead(pass_over, step, c, 1)
            ahead(pass_on, step, c, 2)
            lax.fori_loop(branches // 2, branches, over, 0)
        return carry

    lax.fori_loop(1, spots, phase, 0)

    def drain_attn(b, carry):
        for g in range(groups):
            attn_copy(b, g).wait_send()
        return carry

    lax.fori_loop(0, branches, drain_attn, 0)

    def drain_weight(step, carry):
        for c in range(pieces):
            to_mate(step, c).wait_send()
            for k in range(1, chips):
                to_chip(step, c, k).wait_send()
            for k in range(chips):
                to_core(step, c, k).wait_send()
        return carry

    lax.fori_loop(0, spots, drain_weight, 0)

    def drain_chunks(step, carry):
        def over(b, inner):
            for c in range(halves):
                chunk_copy(step, b, c).wait_send()
            return inner

        return lax.fori_loop(0, branches, over, carry)

    lax.fori_loop(0, spots - 1, drain_chunks, 0)
    for k in range(1, chips):
        across(k).wait_send()
    for k in range(chips):
        beside(k).wait_send()
    for k in range(1, spots):
        to_row(k).wait_send()
    to_side.wait_send()
    for part in range(ratio):
        home_local(part).wait()
        for k in range(1, n_pre):
            to_home(k, part).wait_send()
            to_home(k, part).wait_recv()


def settle_kernel(*refs):
    count = (len(refs) - 1) // 2
    sem = refs[-1]
    copies = [
        pltpu.make_async_copy(refs[i], refs[count + i], sem.at[i]) for i in range(count)
    ]
    for copy in copies:
        copy.start()
    for copy in copies:
        copy.wait()


def settle(*arrays):
    anywhere = pl.BlockSpec(memory_space=pl.ANY)
    return pl.pallas_call(
        settle_kernel,
        out_shape=tuple(jax.ShapeDtypeStruct(a.shape, a.dtype) for a in arrays),
        in_specs=[anywhere] * len(arrays),
        out_specs=(anywhere,) * len(arrays),
        scratch_shapes=[pltpu.SemaphoreType.DMA((len(arrays),))],
        name="settle",
    )(*arrays)


def layer(lists, reach, owner, kv, pool, queries, own, weight, n_pre, n_dec):
    branches, page_len, depth = queries.shape
    count = pool.shape[0]
    cols = weight.shape[1] // n_dec
    ratio = n_dec // n_pre
    chips = n_pre // 2
    spots = n_dec // 2
    groups = depth // (PAIR * HD)
    bf16 = jnp.bfloat16
    anywhere = pl.BlockSpec(memory_space=pl.ANY)
    dma = pltpu.SemaphoreType.DMA
    return pl.pallas_call(
        functools.partial(layer_kernel, n_pre, n_dec),
        out_shape=(
            pltpu.VMEM((branches, page_len, cols), bf16),
            pltpu.VMEM((n_pre, page_len, ratio * kv.shape[2]), bf16),
        ),
        in_specs=[SMEM] * 3 + [VMEM] + [anywhere] * 4,
        out_specs=(VMEM, VMEM),
        scratch_shapes=[
            pltpu.VMEM((count * n_pre,) + pool.shape[1:], bf16),
            pltpu.VMEM(queries.shape, bf16),
            pltpu.VMEM(own.shape, bf16),
            pltpu.VMEM((count * n_pre * page_len, 2 * HD), bf16),
            pltpu.VMEM((branches, page_len, 2 * depth), bf16),
            pltpu.VMEM((spots, 2 * depth, cols), bf16),
            pltpu.VMEM((spots, branches, page_len, cols), bf16),
            pltpu.VMEM((spots + 1, branches, page_len, cols), bf16),
            pltpu.VMEM((branches, 1, count * n_pre * page_len), jnp.float32),
            pltpu.VMEM((spots, 2) + kv.shape[1:], bf16),
            pltpu.VMEM((spots, 2) + kv.shape[1:], bf16),
            pltpu.VMEM((2, spots) + kv.shape[1:], bf16),
            dma((3,)),
            dma((spots,)),
            dma((n_pre,)),
            dma((n_pre,)),
            dma((spots,)),
            dma((spots,)),
            dma((1,)),
            dma((2,)),
            dma((n_pre, ratio)),
            dma((n_pre, ratio)),
            dma((branches, groups)),
            dma((branches, groups)),
            dma((spots, WPIECES)),
            dma((spots, WPIECES)),
            dma((spots, WPIECES, chips)),
            dma((spots, WPIECES, chips)),
            dma((spots, WPIECES, chips)),
            dma((spots, WPIECES, chips)),
            dma((spots, branches, CHUNKS)),
            dma((spots + 1, branches, CHUNKS)),
        ],
        compiler_params=pltpu.CompilerParams(
            has_side_effects=True, collective_id=0, vmem_limit_bytes=62 * 2**20
        ),
        name="layer",
    )(lists, reach, owner, kv, pool, queries, own, weight)


def on_device(
    queries, branch_kv, pool_kv, page_lists, anc_len, dec_owner, output_projection_weight
):
    n_pre = lax.axis_size("pre")
    n_dec = lax.axis_size("dec")
    dec_idx = lax.axis_index("dec")
    kv_cols = pool_kv.shape[2]
    if kv_cols < 2 * HD:
        other_pool, other_own = from_partner((pool_kv, branch_kv), "dec", 0)
        first_half = dec_idx % 2 == 0
        pool = jnp.where(
            first_half,
            jnp.concatenate([pool_kv, other_pool], 2),
            jnp.concatenate([other_pool, pool_kv], 2),
        )
        own = jnp.where(
            first_half,
            jnp.concatenate([branch_kv, other_own], 2),
            jnp.concatenate([other_own, branch_kv], 2),
        )
    else:
        pool, own = pool_kv, branch_kv

    layer_out, decode_pages = layer(
        page_lists,
        anc_len,
        dec_owner,
        branch_kv,
        pool,
        queries,
        own,
        output_projection_weight,
        n_pre,
        n_dec,
    )
    return (layer_out, decode_pages)


def solution(mesh):
    in_specs = (
        P("pre", None, "dec"),
        P("pre", None, "dec"),
        P("pre", None, "dec"),
        P(),
        P(),
        P(),
        P("dec", None),
    )
    out_specs = (P("pre", None, "dec"), P("dec", None, "pre"))
    return jax.shard_map(
        on_device, mesh=mesh, in_specs=in_specs, out_specs=out_specs, check_vma=False
    )
```

time: 134 us -> 119 us (0.89)
  Pallas kernels: 124 us -> 116 us
  local copies, waits for them, and re-layouts: 6.62 us -> 1.77 us
  other arithmetic: 2.64 us -> 0 us
    pallas_call x1, Pallas kernels: 124 us -> 116 us  [layer(): pl.pallas_call(functools.partial(layer_kernel, n_pre, n_dec), out_shape=(...]
    unnamed x2, local copies, waits for them, and re-layouts: 4.13 us -> 1.77 us
    select_n x2 -> x0, other arithmetic: 1.7 us -> none  [the longest x1 1.05 us: on_device(): buckets = jnp.where(onehot[b][:, None, None], branch_kv[b][None], buckets)]
    dynamic_slice x2 -> x0, local copies, waits for them, and re-layouts: 1.46 us -> none  [the longest x1 0.73 us: on_device(): my_counts = lax.dynamic_slice_in_dim(anc_len, start, branch_count, 0)]
where the time goes in v1:
time: 119 us
  Pallas kernels  116 us (97%)
  local copies, waits for them, and re-layouts  1.77 us (1%)
    pallas_call x1, Pallas kernels, layer(): pl.pallas_call(functools.partial(layer_kernel, n_pre, n_dec), out_shape=(...  116 us

profile of v1, /device:TPU:0, one launch (start us, length us, event | category | flops | bytes accessed | tf_op | source)
XLA Modules:
  0.0 118.8 jit_solution(15364410228758944097)
XLA Ops:
  0.6 116.3 %layer.1 = (bf16[4,128,1024]{2,1,0:T(8,128)(2,1)S(1)}, bf16[4,128,512]{2,1,0:T(8,128)(2,1)S(1)}) custom-call(s32[16,16]{1,0:T(8,128)} %lists_ref.1, s32[16]{0:T(128)} %reach_ref.1, s32[16]{0:T(128)} %owner_ref.1, bf16[4,128,256]{2,1,0:T(8,128)(2,1)} %own_hbm.1, bf16[4,128,256]{2,1,0:T(8,128)(2,1)} %pool_ref.1, bf16[4,128,1024]{2,1,0:T(8,128)(2,1)} %q_hbm.1, ...), custom_call_target="tpu_custom_call" | custom-call | tf_op jit(solution)/shard_map/layer/pallas_call | solution.py:623
  117.0 1.0 copy.11
  118.0 0.8 copy.12

commit v2 on v1

--- a/solution.py
+++ b/solution.py
@@ -31,7 +31,7 @@
     values[:, HD:] = jnp.ones((pages * page_len, HD), values.dtype)
 
 
-def attend(branch, first, last, q_ref, own_ref, pool_ref, bias_ref, values, attn, after):
+def attend(branch, g, q_ref, own_ref, pool_ref, bias_ref, values, attn):
     pages, page_len, _ = pool_ref.shape
     keys = pool_ref[:, :, :HD].reshape(pages * page_len, HD)
     own_keys = own_ref[branch, :, :HD]
@@ -43,28 +43,22 @@
     causal = jnp.concatenate([causal] * PAIR, 0)
     bias = bias_ref[branch]
     nt = (((1,), (1,)), ((), ()))
-
-    def group(g, carry):
-        start = pl.multiple_of(g * PAIR * HD, PAIR * HD)
-        q = q_ref[branch, :, pl.ds(start, PAIR * HD)]
-        q = jnp.concatenate([q[:, i * HD : (i + 1) * HD] for i in range(PAIR)], 0)
-        far = lax.dot_general(q, keys, nt, preferred_element_type=jnp.float32) + bias
-        near = lax.dot_general(q, own_keys, nt, preferred_element_type=jnp.float32) + causal
-        top = jnp.maximum(
-            jnp.max(far, axis=-1, keepdims=True), jnp.max(near, axis=-1, keepdims=True)
-        )
-        top = top * SCALE
-        far = jnp.exp2(far * SCALE - top).astype(jnp.bfloat16)
-        near = jnp.exp2(near * SCALE - top).astype(jnp.bfloat16)
-        out = jnp.dot(far, values[...], preferred_element_type=jnp.float32)
-        out = out + jnp.dot(near, own_values, preferred_element_type=jnp.float32)
-        out = (out[:, :HD] / out[:, HD:]).astype(jnp.bfloat16)
-        for i in range(PAIR):
-            attn[branch, :, pl.ds(start + i * HD, HD)] = out[i * page_len : (i + 1) * page_len]
-        after(branch, g)
-        return carry
-
-    lax.fori_loop(first, last, group, 0)
+    start = pl.multiple_of(g * PAIR * HD, PAIR * HD)
+    q = q_ref[branch, :, pl.ds(start, PAIR * HD)]
+    q = jnp.concatenate([q[:, i * HD : (i + 1) * HD] for i in range(PAIR)], 0)
+    far = lax.dot_general(q, keys, nt, preferred_element_type=jnp.float32) + bias
+    near = lax.dot_general(q, own_keys, nt, preferred_element_type=jnp.float32) + causal
+    top = jnp.maximum(
+        jnp.max(far, axis=-1, keepdims=True), jnp.max(near, axis=-1, keepdims=True)
+    )
+    top = top * SCALE
+    far = jnp.exp2(far * SCALE - top).astype(jnp.bfloat16)
+    near = jnp.exp2(near * SCALE - top).astype(jnp.bfloat16)
+    out = jnp.dot(far, values[...], preferred_element_type=jnp.float32)
+    out = out + jnp.dot(near, own_values, preferred_element_type=jnp.float32)
+    out = (out[:, :HD] / out[:, HD:]).astype(jnp.bfloat16)
+    for i in range(PAIR):
+        attn[branch, :, pl.ds(start + i * HD, HD)] = out[i * page_len : (i + 1) * page_len]
 
 
 def layer_kernel(
@@ -409,12 +403,12 @@
 
         lax.fori_loop(0, spots, clear, 0)
 
+    pass_on(0, 0)
     for k in range(1, chips):
         across(k).wait_recv()
         beside(k).start()
 
-    for c in range(pieces // 2):
-        pass_on(0, c)
+    pass_on(0, 1)
     for copy in loads:
         copy.wait()
     for k in range(chips):
@@ -427,81 +421,79 @@
 
     lax.fori_loop(1, spots, load_rest, 0)
 
-    def after(b, g):
+    def first_chunks(b):
+        for g in range(groups):
+            attn_copy(b, g).wait_recv()
+        for c in range(halves):
+            @pl.when(b == 0)
+            def _(c=c):
+                for p in range(c * per_half, (c + 1) * per_half):
+                    need(0, p)
+
+            send_chunk(0, b, c)
+
+    total_groups = branches * groups
+
+    def at(n, where):
+        def run(act):
+            @pl.when(n == where)
+            def _():
+                act()
+
+        return run
+
+    def turn(n, carry):
+        b = n // groups
+        g = lax.rem(n, groups)
+        attend(b, g, q_ref, own_ref, all_ref, bias_ref, values, attn)
         attn_copy(b, g).start()
 
-    def some(i, first, last):
-        @pl.when(i < branches)
-        def _():
-            attend(
-                i, first, last, q_ref, own_ref, all_ref, bias_ref, values, attn, after
-            )
-
-    def turn(i, carry):
-        some(i, 0, groups // 2)
-
-        @pl.when(i == 0)
-        def _():
-            for c in range(pieces // 2, pieces):
-                pass_on(0, c)
-            for c in range(pieces // 2):
-                pass_over(0, c)
-
-        @pl.when(i > 0)
-        def _():
-            b = i - 1
-
-            @pl.when(i == 1)
-            def _():
-                own_rows(0).wait()
-
-            for g in range(groups):
-                attn_copy(b, g).wait_recv()
-            for c in range(halves):
-                @pl.when(i == 1)
-                def _(c=c):
-                    for p in range(c * per_half, (c + 1) * per_half):
-                        need(0, p)
-
-                send_chunk(0, b, c)
-
-        some(i, groups // 2, groups)
-
-        @pl.when(i == 0)
-        def _():
-            for c in range(pieces // 2, pieces):
-                pass_over(0, c)
-
-        @pl.when(i == 0)
-        def _():
+        @at(n, 0)
+        def _():
+            pass_on(0, 2)
+            pass_over(0, 0)
+
+        @at(n, 2)
+        def _():
+            pass_on(0, 3)
+            pass_over(0, 1)
+
+        @at(n, 4)
+        def _():
+            pass_over(0, 2)
             to_mate(1, 0).start()
 
-        @pl.when(i == 2)
+        @at(n, 5)
+        def _():
+            own_rows(0).wait()
+            pass_over(0, 3)
+
+        @pl.when(jnp.logical_and(n >= groups, g == groups // 2 - 1))
+        def _():
+            first_chunks(b - 1)
+
+        @at(n, 11)
         def _():
             to_mate(1, 1).start()
-            pages_to_side()
-
-        @pl.when(i == branches - 1)
+            pass_on(1, 0)
+
+        @at(n, total_groups - 1)
         def _():
             for c in range(2, pieces):
                 to_mate(1, c).start()
             if spots > 2:
                 for c in range(pieces):
                     to_mate(2, c).start()
-            for c in range(per_half):
-                pass_on(1, c)
-
-        @pl.when(i == branches)
-        def _():
-            pages_to_home()
-            for c in range(per_half):
-                pass_over(1, c)
-            for c in range(per_half, pieces):
-                pass_on(1, c)
+            pass_on(1, 1)
+            pass_over(1, 0)
 
         return carry
 
-    lax.fori_loop(0, branches + 1, turn, 0)
+    lax.fori_loop(0, total_groups, turn, 0)
+    first_chunks(branches - 1)
+    pass_over(1, 1)
+    for c in range(per_half, pieces):
+        pass_on(1, c)
 
     def ahead(act, step, c, by):
         later = c + by
@@ -520,6 +512,14 @@
         def _():
             for p in range(pieces):
                 to_mate(step + 2, p).start()
+
+        @pl.when(step == spots - 2)
+        def _():
+            pages_to_side()
+
+        @pl.when(step == spots - 1)
+        def _():
+            pages_to_home()
 
         for c in range(halves):
             for p in range(c * per_half, (c + 1) * per_half):

time: 119 us -> 110 us (0.924)
  Pallas kernels: 116 us -> 108 us
    pallas_call x1, Pallas kernels: 116 us -> 108 us  [layer(): pl.pallas_call(functools.partial(layer_kernel, n_pre, n_dec), out_shape=(...]
where the time goes in v2:
time: 110 us
  Pallas kernels  108 us (98%)
  local copies, waits for them, and re-layouts  1.77 us (2%)
    pallas_call x1, Pallas kernels, layer(): pl.pallas_call(functools.partial(layer_kernel, n_pre, n_dec), out_shape=(...  108 us

profile of v2, /device:TPU:0, one launch (start us, length us, event | category | flops | bytes accessed | tf_op | source)
XLA Modules:
  0.0 110.1 jit_solution(10199214489057345203)
XLA Ops:
  0.6 107.7 %layer.1 = (bf16[4,128,1024]{2,1,0:T(8,128)(2,1)S(1)}, bf16[4,128,512]{2,1,0:T(8,128)(2,1)S(1)}) custom-call(s32[16,16]{1,0:T(8,128)} %lists_ref.1, s32[16]{0:T(128)} %reach_ref.1, s32[16]{0:T(128)} %owner_ref.1, bf16[4,128,256]{2,1,0:T(8,128)(2,1)} %own_hbm.1, bf16[4,128,256]{2,1,0:T(8,128)(2,1)} %pool_ref.1, bf16[4,128,1024]{2,1,0:T(8,128)(2,1)} %q_hbm.1, ...), custom_call_target="tpu_custom_call" | custom-call | tf_op jit(solution)/shard_map/layer/pallas_call | solution.py:623
  108.3 1.0 copy.11
  109.3 0.8 copy.12

commit v3 on v2

--- a/solution.py
+++ b/solution.py
@@ -15,8 +15,8 @@
 VMEM = pl.BlockSpec(memory_space=pltpu.VMEM)
 SMEM = pl.BlockSpec(memory_space=pltpu.SMEM)
 PAIR = 2
-WPIECES = 4
-CHUNKS = 2
+BLOCK = 2
+PIECES = 4
 
 
 def from_partner(value, axis, stride):
@@ -31,7 +31,7 @@
     values[:, HD:] = jnp.ones((pages * page_len, HD), values.dtype)
 
 
-def attend(branch, g, q_ref, own_ref, pool_ref, bias_ref, values, attn):
+def attend(branch, start, block, q_ref, own_ref, pool_ref, bias_ref, values, attn):
     pages, page_len, _ = pool_ref.shape
     keys = pool_ref[:, :, :HD].reshape(pages * page_len, HD)
     own_keys = own_ref[branch, :, :HD]
@@ -43,22 +43,24 @@
     causal = jnp.concatenate([causal] * PAIR, 0)
     bias = bias_ref[branch]
     nt = (((1,), (1,)), ((), ()))
-    start = pl.multiple_of(g * PAIR * HD, PAIR * HD)
-    q = q_ref[branch, :, pl.ds(start, PAIR * HD)]
-    q = jnp.concatenate([q[:, i * HD : (i + 1) * HD] for i in range(PAIR)], 0)
-    far = lax.dot_general(q, keys, nt, preferred_element_type=jnp.float32) + bias
-    near = lax.dot_general(q, own_keys, nt, preferred_element_type=jnp.float32) + causal
-    top = jnp.maximum(
-        jnp.max(far, axis=-1, keepdims=True), jnp.max(near, axis=-1, keepdims=True)
-    )
-    top = top * SCALE
-    far = jnp.exp2(far * SCALE - top).astype(jnp.bfloat16)
-    near = jnp.exp2(near * SCALE - top).astype(jnp.bfloat16)
-    out = jnp.dot(far, values[...], preferred_element_type=jnp.float32)
-    out = out + jnp.dot(near, own_values, preferred_element_type=jnp.float32)
-    out = (out[:, :HD] / out[:, HD:]).astype(jnp.bfloat16)
-    for i in range(PAIR):
-        attn[branch, :, pl.ds(start + i * HD, HD)] = out[i * page_len : (i + 1) * page_len]
+    outs = []
+    for g in range(block):
+        q = q_ref[branch, :, pl.ds(start + g * PAIR * HD, PAIR * HD)]
+        q = jnp.concatenate([q[:, i * HD : (i + 1) * HD] for i in range(PAIR)], 0)
+        far = lax.dot_general(q, keys, nt, preferred_element_type=jnp.float32) + bias
+        near = lax.dot_general(q, own_keys, nt, preferred_element_type=jnp.float32) + causal
+        top = jnp.maximum(
+            jnp.max(far, axis=-1, keepdims=True), jnp.max(near, axis=-1, keepdims=True)
+        )
+        top = top * SCALE
+        far = jnp.exp2(far * SCALE - top).astype(jnp.bfloat16)
+        near = jnp.exp2(near * SCALE - top).astype(jnp.bfloat16)
+        out = jnp.dot(far, values[...], preferred_element_type=jnp.float32)
+        out = out + jnp.dot(near, own_values, preferred_element_type=jnp.float32)
+        out = (out[:, :HD] / out[:, HD:]).astype(jnp.bfloat16)
+        outs.extend(out[i * page_len : (i + 1) * page_len] for i in range(PAIR))
+    for i, out in enumerate(outs):
+        attn[branch, :, pl.ds(start + i * HD, HD)] = out
 
 
 def layer_kernel(
@@ -122,19 +124,18 @@
     side = lax.rem(dec, 2)
     mate = dec + 1 - 2 * side
     share = depth // n_pre
-    pieces = WPIECES
+    pieces = PIECES
     piece = cols // pieces
-    halves = CHUNKS
-    half = cols // halves
-    per_half = pieces // halves
-    groups = depth // (PAIR * HD)
+    block = min(BLOCK, depth // (PAIR * HD))
+    span = block * PAIR * HD
+    blocks = depth // span
     low = 2 * spot < spots
 
     def target(step):
-        outer = spots - 1 - spot
-        rising = jnp.where(step < outer, spots - 1 - step, step - outer)
-        falling = jnp.where(step < spot, step, spots - 1 - step + spot)
-        return jnp.where(low, rising, falling)
+        near = jnp.where(low, spot, spots - 1 - spot)
+        paired = jnp.where(step % 2 == 0, spots - 1 - step // 2, step // 2)
+        t = jnp.where(step < 2 * near, paired, spots - 1 - step + near)
+        return jnp.where(low, t, spots - 1 - t)
 
     def block_of(device):
         return pl.ds(device * count, count)
@@ -220,21 +221,21 @@
             to_core(step, c, k).wait_recv()
 
     def attn_copy(b, g):
-        start = pl.multiple_of(g * PAIR * HD, PAIR * HD)
-        return pltpu.make_async_remote_copy(
-            src_ref=attn.at[b, :, pl.ds(start, PAIR * HD)],
-            dst_ref=attn.at[b, :, pl.ds(depth + start, PAIR * HD)],
+        start = pl.multiple_of(g * span, span)
+        return pltpu.make_async_remote_copy(
+            src_ref=attn.at[b, :, pl.ds(start, span)],
+            dst_ref=attn.at[b, :, pl.ds(depth + start, span)],
             send_sem=asend.at[b, g],
             recv_sem=arecv.at[b, g],
             device_id={"dec": mate},
             device_id_type=MESH,
         )
 
-    def at_half(c):
-        return pl.ds(pl.multiple_of(c * half, half), half)
+    def at_piece(c):
+        return pl.ds(pl.multiple_of(c * piece, piece), piece)
 
     def arrival(slot, b, c):
-        where = got.at[slot, b, :, at_half(c)]
+        where = got.at[slot, b, :, at_piece(c)]
         return pltpu.make_async_copy(where, where, rsem.at[slot, b, c])
 
     def chunk_copy(step, b, c):
@@ -242,8 +243,8 @@
         onward = t > spot
         slot = jnp.where(t == spot - 1, spots, t)
         return pltpu.make_async_remote_copy(
-            src_ref=sent.at[t, b, :, at_half(c)],
-            dst_ref=got.at[slot, b, :, at_half(c)],
+            src_ref=sent.at[t, b, :, at_piece(c)],
+            dst_ref=got.at[slot, b, :, at_piece(c)],
             send_sem=ssem.at[step, b, c],
             recv_sem=rsem.at[slot, b, c],
             device_id={"dec": jnp.where(onward, dec + 2, dec - 2)},
@@ -258,9 +259,9 @@
         def _():
             arrival(t, b, c).wait()
 
-        total = jnp.dot(attn[b], wv[t, :, at_half(c)], preferred_element_type=jnp.float32)
-        total = total + got[t, b, :, at_half(c)].astype(jnp.float32)
-        sent[t, b, :, at_half(c)] = total.astype(jnp.bfloat16)
+        total = jnp.dot(attn[b], wv[t, :, at_piece(c)], preferred_element_type=jnp.float32)
+        total = total + got[t, b, :, at_piece(c)].astype(jnp.float32)
+        sent[t, b, :, at_piece(c)] = total.astype(jnp.bfloat16)
         chunk_copy(step, b, c).start()
 
     def last_chunk(b, c):
@@ -272,10 +273,10 @@
         def _():
             arrival(spots, b, c).wait()
 
-        total = jnp.dot(attn[b], wv[spot, :, at_half(c)], preferred_element_type=jnp.float32)
-        total = total + got[spot, b, :, at_half(c)].astype(jnp.float32)
-        total = total + got[spots, b, :, at_half(c)].astype(jnp.float32)
-        out_ref[b, :, at_half(c)] = total.astype(jnp.bfloat16)
+        total = jnp.dot(attn[b], wv[spot, :, at_piece(c)], preferred_element_type=jnp.float32)
+        total = total + got[spot, b, :, at_piece(c)].astype(jnp.float32)
+        total = total + got[spots, b, :, at_piece(c)].astype(jnp.float32)
+        out_ref[b, :, at_piece(c)] = total.astype(jnp.bfloat16)
 
     def to_row(k):
         where = lax.rem(spot + k, spots)
@@ -421,18 +422,8 @@
 
     lax.fori_loop(1, spots, load_rest, 0)
 
-    def first_chunks(b):
-        for g in range(groups):
-            attn_copy(b, g).wait_recv()
-        for c in range(halves):
-            @pl.when(b == 0)
-            def _(c=c):
-                for p in range(c * per_half, (c + 1) * per_half):
-                    need(0, p)
-
-            send_chunk(0, b, c)
-
-    total_groups = branches * groups
+    total = branches * blocks
+    last = branches - 1
 
     def at(n, where):
         def run(act):
@@ -442,10 +433,23 @@
 
         return run
 
+    def first_chunks(b, carry):
+        for g in range(blocks):
+            attn_copy(b, g).wait_recv()
+        for c in range(pieces):
+            send_chunk(0, b, c)
+        return carry
+
     def turn(n, carry):
-        b = n // groups
-        g = lax.rem(n, groups)
-        attend(b, g, q_ref, own_ref, all_ref, bias_ref, values, attn)
+        b = n // blocks
+        g = lax.rem(n, blocks)
+        start = pl.multiple_of(g * span, span)
+        attend(b, start, block, q_ref, own_ref, all_ref, bias_ref, values, attn)
+
+        @at(n, last * blocks)
+        def _():
+            to_mate(1, 0).start()
+
         attn_copy(b, g).start()
 
         @at(n, 0)
@@ -461,91 +465,88 @@
         @at(n, 4)
         def _():
             pass_over(0, 2)
-            to_mate(1, 0).start()
-
-        @at(n, 5)
-        def _():
+
+        @at(n, 6)
+        def _():
+            pass_over(0, 3)
             own_rows(0).wait()
-            pass_over(0, 3)
-
-        @pl.when(jnp.logical_and(n >= groups, g == groups // 2 - 1))
-        def _():
-            first_chunks(b - 1)
-
-        @at(n, 11)
-        def _():
-            to_mate(1, 1).start()
-            pass_on(1, 0)
-
-        @at(n, total_groups - 1)
-        def _():
-            for c in range(2, pieces):
-                to_mate(1, c).start()
-            if spots > 2:
-                for c in range(pieces):
-                    to_mate(2, c).start()
-            pass_on(1, 1)
-            pass_over(1, 0)
+            for c in range(pieces):
+                need(0, c)
+            first_chunks(0, 0)
 
         return carry
 
-    lax.fori_loop(0, total_groups, turn, 0)
-    first_chunks(branches - 1)
+    lax.fori_loop(0, total, turn, 0)
+    for c in range(1, pieces):
+        to_mate(1, c).start()
+    if spots > 2:
+        for c in range(pieces):
+            to_mate(2, c).start()
+    lax.fori_loop(1, last, first_chunks, 0)
+    own_rows(1).wait()
+    pass_on(1, 0)
+    pass_over(1, 0)
+    need(1, 0)
+
+    def second_chunk(b, carry):
+        send_chunk(1, b, 0)
+        return carry
+
+    lax.fori_loop(0, last, second_chunk, 0)
+    first_chunks(last, 0)
+    second_chunk(last, 0)
+    pass_on(1, 1)
+    pass_on(1, 2)
     pass_over(1, 1)
-    for c in range(per_half, pieces):
-        pass_on(1, c)
+    pass_on(1, 3)
 
     def ahead(act, step, c, by):
-        later = c + by
-        where = step + later // halves
-        first = later % halves * per_half
+        where = step + (c + by) // pieces
 
         @pl.when(where < spots)
         def _():
-            for p in range(first, first + per_half):
-                act(where, p)
+            act(where, (c + by) % pieces)
+
+    def column(step, c, act):
+        need(step, c)
+
+        def over(b, carry):
+            act(b, c)
+            return carry
+
+        lax.fori_loop(0, branches, over, 0)
+        ahead(pass_over, step, c, 1)
+        ahead(pass_on, step, c, 3)
 
     def phase(step, carry):
-        own_rows(step).wait()
-
-        @pl.when(step + 2 < spots)
-        def _():
-            for p in range(pieces):
-                to_mate(step + 2, p).start()
-
-        @pl.when(step == spots - 2)
-        def _():
-            pages_to_side()
-
-        @pl.when(step == spots - 1)
-        def _():
-            pages_to_home()
-
-        for c in range(halves):
-            for p in range(c * per_half, (c + 1) * per_half):
-                need(step, p)
-
-            def over(b, inner, c=c):
-                @pl.when(step < spots - 1)
+        for c in range(pieces):
+            if c == 0:
+                @pl.when(step > 1)
                 def _():
-                    send_chunk(step, b, c)
-
-                @pl.when(step == spots - 1)
+                    own_rows(step).wait()
+                    column(step, 0, functools.partial(send_chunk, step))
+            else:
+                column(step, c, functools.partial(send_chunk, step))
+            if c == 1:
+                @pl.when(step + 2 < spots)
                 def _():
-                    last_chunk(b, c)
-
-                return inner
-
-            lax.fori_loop(0, branches // 2, over, 0)
-            ahead(pass_over, step, c, 1)
-            ahead(pass_on, step, c, 2)
-            lax.fori_loop(branches // 2, branches, over, 0)
+                    for p in range(pieces):
+                        to_mate(step + 2, p).start()
+
+                @pl.when(step == spots - 2)
+                def _():
+                    pages_to_side()
+
         return carry
 
-    lax.fori_loop(1, spots, phase, 0)
+    lax.fori_loop(1, spots - 1, phase, 0)
+    own_rows(spots - 1).wait()
+    pages_to_home()
+    for c in range(pieces):
+        column(spots - 1, c, last_chunk)
 
     def drain_attn(b, carry):
-        for g in range(groups):
+        for g in range(blocks):
             attn_copy(b, g).wait_send()
         return carry
 
@@ -564,7 +565,7 @@
 
     def drain_chunks(step, carry):
         def over(b, inner):
-            for c in range(halves):
+            for c in range(pieces):
                 chunk_copy(step, b, c).wait_send()
             return inner
 
@@ -616,7 +617,7 @@
     ratio = n_dec // n_pre
     chips = n_pre // 2
     spots = n_dec // 2
-    groups = depth // (PAIR * HD)
+    blocks = depth // (min(BLOCK, depth // (PAIR * HD)) * PAIR * HD)
     bf16 = jnp.bfloat16
     anywhere = pl.BlockSpec(memory_space=pl.ANY)
     dma = pltpu.SemaphoreType.DMA
@@ -651,16 +652,16 @@
             dma((2,)),
             dma((n_pre, ratio)),
             dma((n_pre, ratio)),
-            dma((branches, groups)),
-            dma((branches, groups)),
-            dma((spots, WPIECES)),
-            dma((spots, WPIECES)),
-            dma((spots, WPIECES, chips)),
-            dma((spots, WPIECES, chips)),
-            dma((spots, WPIECES, chips)),
-            dma((spots, WPIECES, chips)),
-            dma((spots, branches, CHUNKS)),
-            dma((spots + 1, branches, CHUNKS)),
+            dma((branches, blocks)),
+            dma((branches, blocks)),
+            dma((spots, PIECES)),
+            dma((spots, PIECES)),
+            dma((spots, PIECES, chips)),
+            dma((spots, PIECES, chips)),
+            dma((spots, PIECES, chips)),
+            dma((spots, PIECES, chips)),
+            dma((spots, branches, PIECES)),
+            dma((spots + 1, branches, PIECES)),
         ],
         compiler_params=pltpu.CompilerParams(
             has_side_effects=True, collective_id=0, vmem_limit_bytes=62 * 2**20

time: 110 us -> 105 us (0.955); the launches traced: 110 us -> 103 us
  Pallas kernels: 108 us -> 101 us
    pallas_call x1, Pallas kernels: 108 us -> 101 us  [layer(): pl.pallas_call(functools.partial(layer_kernel, n_pre, n_dec), out_shape=(...]
where the time goes in v3:
time: 105 us; the launch traced here: 103 us
  Pallas kernels  101 us (96%)
  local copies, waits for them, and re-layouts  1.77 us (2%)
    pallas_call x1, Pallas kernels, layer(): pl.pallas_call(functools.partial(layer_kernel, n_pre, n_dec), out_shape=(...  101 us

profile of v3, /device:TPU:0, one launch (start us, length us, event | category | flops | bytes accessed | tf_op | source)
XLA Modules:
  0.0 103.4 jit_solution(4744150081647162579)
XLA Ops:
  0.6 101.0 %layer.1 = (bf16[4,128,1024]{2,1,0:T(8,128)(2,1)S(1)}, bf16[4,128,512]{2,1,0:T(8,128)(2,1)S(1)}) custom-call(s32[16,16]{1,0:T(8,128)} %lists_ref.1, s32[16]{0:T(128)} %reach_ref.1, s32[16]{0:T(128)} %owner_ref.1, bf16[4,128,256]{2,1,0:T(8,128)(2,1)} %own_hbm.1, bf16[4,128,256]{2,1,0:T(8,128)(2,1)} %pool_ref.1, bf16[4,128,1024]{2,1,0:T(8,128)(2,1)} %q_hbm.1, ...), custom_call_target="tpu_custom_call" | custom-call | tf_op jit(solution)/shard_map/layer/pallas_call | solution.py:624
  101.7 1.0 copy.11
  102.6 0.8 copy.12

commit v4 on v3

--- a/solution.py
+++ b/solution.py
@@ -13,7 +13,6 @@
 SCALE = HD**-0.5 * math.log2(math.e)
 MESH = pl.DeviceIdType.MESH
 VMEM = pl.BlockSpec(memory_space=pltpu.VMEM)
-SMEM = pl.BlockSpec(memory_space=pltpu.SMEM)
 PAIR = 2
 BLOCK = 2
 PIECES = 4
@@ -66,10 +65,10 @@
 def layer_kernel(
     n_pre,
     n_dec,
-    lists_ref,
-    reach_ref,
-    owner_ref,
-    kv_ref,
+    lists_hbm,
+    reach_hbm,
+    owner_hbm,
+    kv_hbm,
     pool_ref,
     q_hbm,
     own_hbm,
@@ -88,6 +87,14 @@
     bucket_ref,
     row_ref,
     block_ref,
+    lists_ref,
+    reach_ref,
+    owner_ref,
+    kv_ref,
+    far_weight,
+    far_sent,
+    far_land,
+    far_got,
     load_sem,
     wsem,
     psend,
@@ -106,8 +113,12 @@
     xrecv,
     csend,
     crecv,
+    greet,
     ssem,
     rsem,
+    fsend,
+    frecv,
+    gsem,
 ):
     pre = lax.axis_index("pre")
     dec = lax.axis_index("dec")
@@ -130,6 +141,8 @@
     span = block * PAIR * HD
     blocks = depth // span
     low = 2 * spot < spots
+    outer = jnp.logical_or(spot == 0, spot == spots - 1)
+    across_end = spots - 1 - spot
 
     def target(step):
         near = jnp.where(low, spot, spots - 1 - spot)
@@ -231,6 +244,32 @@
             device_id_type=MESH,
         )
 
+    def far_rows():
+        start = pl.multiple_of((2 * across_end + 1 - side) * cols, cols)
+        return pltpu.make_async_copy(
+            w_ref.at[:, pl.ds(start, cols)], far_weight, load_sem.at[7]
+        )
+
+    def far_copy(c):
+        return pltpu.make_async_remote_copy(
+            src_ref=far_sent.at[:, at_piece(c)],
+            dst_ref=far_land.at[:, at_piece(c)],
+            send_sem=fsend.at[c],
+            recv_sem=frecv.at[c],
+            device_id={"dec": 2 * across_end + side},
+            device_id_type=MESH,
+        )
+
+    def far_give():
+        return pltpu.make_async_remote_copy(
+            src_ref=far_land,
+            dst_ref=far_got,
+            send_sem=gsem.at[0],
+            recv_sem=gsem.at[1],
+            device_id={"dec": mate},
+            device_id_type=MESH,
+        )
+
     def at_piece(c):
         return pl.ds(pl.multiple_of(c * piece, piece), piece)
 
@@ -277,6 +316,11 @@
         total = total + got[spot, b, :, at_piece(c)].astype(jnp.float32)
         total = total + got[spots, b, :, at_piece(c)].astype(jnp.float32)
         out_ref[b, :, at_piece(c)] = total.astype(jnp.bfloat16)
+
+        @pl.when(jnp.logical_and(outer, b == 0))
+        def _():
+            whole = total + far_got[:, at_piece(c)].astype(jnp.float32)
+            out_ref[b, :, at_piece(c)] = whole.astype(jnp.bfloat16)
 
     def to_row(k):
         where = lax.rem(spot + k, spots)
@@ -342,34 +386,64 @@
             barrier, 1, device_id={"pre": lax.rem(pre + k, n_pre)}, device_id_type=MESH
         )
     pl.semaphore_signal(barrier, 1, device_id={"dec": mate}, device_id_type=MESH)
-    for k in range(1, spots):
-        pl.semaphore_signal(
-            barrier,
-            1,
-            device_id={"dec": 2 * lax.rem(spot + k, spots) + side},
-            device_id_type=MESH,
-        )
+    def signal_along(above, below):
+        @pl.when(spot < spots - 1)
+        def _():
+            pl.semaphore_signal(above, 1, device_id={"dec": dec + 2}, device_id_type=MESH)
+
+        @pl.when(spot > 0)
+        def _():
+            pl.semaphore_signal(below, 1, device_id={"dec": dec - 2}, device_id_type=MESH)
+
+    def greet_further():
+        for k in range(spots - 2):
+            signal_along(greet.at[0, k], greet.at[1, k])
+
+            @pl.when(spot > 0)
+            def _(k=k):
+                pl.semaphore_wait(greet.at[0, k], 1)
+
+            @pl.when(spot < spots - 1)
+            def _(k=k):
+                pl.semaphore_wait(greet.at[1, k], 1)
+
+    signal_along(barrier, barrier)
     loads = [
         pltpu.make_async_copy(pool_ref, all_ref.at[block_of(pre)], load_sem.at[0]),
         pltpu.make_async_copy(q_hbm, q_ref, load_sem.at[1]),
         pltpu.make_async_copy(own_hbm, own_ref, load_sem.at[2]),
     ]
-    for copy in loads:
+    tables = [
+        pltpu.make_async_copy(owner_hbm, owner_ref, load_sem.at[3]),
+        pltpu.make_async_copy(kv_hbm, kv_ref, load_sem.at[4]),
+        pltpu.make_async_copy(lists_hbm, lists_ref, load_sem.at[5]),
+        pltpu.make_async_copy(reach_hbm, reach_ref, load_sem.at[6]),
+    ]
+    for copy in tables + loads:
         copy.start()
     own_rows(0).start()
-    pl.semaphore_wait(barrier, n_pre + spots - 1)
+
+    @pl.when(outer)
+    def _():
+        far_rows().start()
+
+    pl.semaphore_wait(barrier, n_pre + jnp.minimum(spot, 1) + jnp.minimum(spots - 1 - spot, 1))
 
     for k in range(1, chips):
         across(k).start()
     beside(0).start()
     for c in range(pieces):
         to_mate(0, c).start()
+    to_mate(1, 0).start()
+    for copy in tables:
+        copy.wait()
     first = pre * branches
     for o in range(n_dec):
         bucket = jnp.zeros(kv_ref.shape[1:], kv_ref.dtype)
         for b in range(branches):
             bucket = jnp.where(owner_ref[first + b] == o, kv_ref[b], bucket)
         bucket_ref[o // 2, o % 2] = bucket
+    greet_further()
     for k in range(1, spots):
         to_row(k).start()
     row_local.start()
@@ -423,7 +497,6 @@
     lax.fori_loop(1, spots, load_rest, 0)
 
     total = branches * blocks
-    last = branches - 1
 
     def at(n, where):
         def run(act):
@@ -433,12 +506,32 @@
 
         return run
 
-    def first_chunks(b, carry):
+    def gathered(b):
         for g in range(blocks):
             attn_copy(b, g).wait_recv()
+
+    def first_chunks(b, carry):
+        gathered(b)
         for c in range(pieces):
             send_chunk(0, b, c)
         return carry
+
+    def second_chunk(b, carry):
+        send_chunk(1, b, 0)
+        return carry
+
+    def own_chunks():
+        mine = attn[0, :, :depth]
+        t = target(0)
+        for c in range(pieces):
+            near = jnp.dot(mine, wv[t, :depth, at_piece(c)], preferred_element_type=jnp.float32)
+            sent[t, 0, :, at_piece(c)] = near.astype(jnp.bfloat16)
+            chunk_copy(0, 0, c).start()
+        far_rows().wait()
+        for c in range(pieces):
+            far = jnp.dot(mine, far_weight[:, at_piece(c)], preferred_element_type=jnp.float32)
+            far_sent[:, at_piece(c)] = far.astype(jnp.bfloat16)
+            far_copy(c).start()
 
     def turn(n, carry):
         b = n // blocks
@@ -446,11 +539,17 @@
         start = pl.multiple_of(g * span, span)
         attend(b, start, block, q_ref, own_ref, all_ref, bias_ref, values, attn)
 
-        @at(n, last * blocks)
-        def _():
-            to_mate(1, 0).start()
-
-        attn_copy(b, g).start()
+        @pl.when(b > 0)
+        def _():
+            attn_copy(b, g).start()
+
+        @at(n, blocks - 1)
+        def _():
+            own_rows(0).wait()
+
+            @pl.when(outer)
+            def _():
+                own_chunks()
 
         @at(n, 0)
         def _():
@@ -462,43 +561,52 @@
             pass_on(0, 3)
             pass_over(0, 1)
 
+        @at(n, 3)
+        def _():
+            pass_on(1, 0)
+
         @at(n, 4)
         def _():
             pass_over(0, 2)
 
+        @at(n, 5)
+        def _():
+            pass_over(0, 3)
+
         @at(n, 6)
         def _():
-            pass_over(0, 3)
-            own_rows(0).wait()
-            for c in range(pieces):
-                need(0, c)
-            first_chunks(0, 0)
+            pass_over(1, 0)
 
         return carry
 
     lax.fori_loop(0, total, turn, 0)
-    for c in range(1, pieces):
+    to_mate(1, 1).start()
+    for g in range(blocks):
+        attn_copy(0, g).start()
+    for c in range(2, pieces):
         to_mate(1, c).start()
     if spots > 2:
         for c in range(pieces):
             to_mate(2, c).start()
-    lax.fori_loop(1, last, first_chunks, 0)
+    for c in range(pieces):
+        need(0, c)
+    lax.fori_loop(1, branches, first_chunks, 0)
     own_rows(1).wait()
-    pass_on(1, 0)
-    pass_over(1, 0)
     need(1, 0)
-
-    def second_chunk(b, carry):
-        send_chunk(1, b, 0)
-        return carry
-
-    lax.fori_loop(0, last, second_chunk, 0)
-    first_chunks(last, 0)
-    second_chunk(last, 0)
+    lax.fori_loop(1, branches, second_chunk, 0)
     pass_on(1, 1)
+    pass_over(1, 1)
+
+    @pl.when(outer)
+    def _():
+        gathered(0)
+
+    @pl.when(jnp.logical_not(outer))
+    def _():
+        first_chunks(0, 0)
+
+    second_chunk(0, 0)
     pass_on(1, 2)
-    pass_over(1, 1)
-    pass_on(1, 3)
 
     def ahead(act, step, c, by):
         where = step + (c + by) // pieces
@@ -515,6 +623,11 @@
             return carry
 
         lax.fori_loop(0, branches, over, 0)
+        if c == 1:
+            @pl.when(step == 1)
+            def _():
+                pass_on(1, 3)
+
         ahead(pass_over, step, c, 1)
         ahead(pass_on, step, c, 3)
 
@@ -535,15 +648,34 @@
 
                 @pl.when(step == spots - 2)
                 def _():
+                    @pl.when(outer)
+                    def _():
+                        for p in range(pieces):
+                            far_copy(p).wait_recv()
+                        far_give().start()
+
                     pages_to_side()
 
         return carry
 
     lax.fori_loop(1, spots - 1, phase, 0)
     own_rows(spots - 1).wait()
-    pages_to_home()
+
+    @pl.when(outer)
+    def _():
+        far_give().wait_recv()
+
     for c in range(pieces):
         column(spots - 1, c, last_chunk)
+        if c == 0:
+            pages_to_home()
+
+    @pl.when(outer)
+    def _():
+        far_give().wait_send()
+        for c in range(pieces):
+            far_copy(c).wait_send()
+
 
     def drain_attn(b, carry):
         for g in range(blocks):
@@ -627,7 +759,7 @@
             pltpu.VMEM((branches, page_len, cols), bf16),
             pltpu.VMEM((n_pre, page_len, ratio * kv.shape[2]), bf16),
         ),
-        in_specs=[SMEM] * 3 + [VMEM] + [anywhere] * 4,
+        in_specs=[anywhere] * 8,
         out_specs=(VMEM, VMEM),
         scratch_shapes=[
             pltpu.VMEM((count * n_pre,) + pool.shape[1:], bf16),
@@ -642,7 +774,15 @@
             pltpu.VMEM((spots, 2) + kv.shape[1:], bf16),
             pltpu.VMEM((spots, 2) + kv.shape[1:], bf16),
             pltpu.VMEM((2, spots) + kv.shape[1:], bf16),
-            dma((3,)),
+            pltpu.SMEM(lists.shape, jnp.int32),
+            pltpu.SMEM(reach.shape, jnp.int32),
+            pltpu.SMEM(owner.shape, jnp.int32),
+            pltpu.VMEM(kv.shape, bf16),
+            pltpu.VMEM((depth, cols), bf16),
+            pltpu.VMEM((page_len, cols), bf16),
+            pltpu.VMEM((page_len, cols), bf16),
+            pltpu.VMEM((page_len, cols), bf16),
+            dma((8,)),
             dma((spots,)),
             dma((n_pre,)),
             dma((n_pre,)),
@@ -660,8 +800,12 @@
             dma((spots, PIECES, chips)),
             dma((spots, PIECES, chips)),
             dma((spots, PIECES, chips)),
+            pltpu.SemaphoreType.REGULAR((2, spots - 2)),
             dma((spots, branches, PIECES)),
             dma((spots + 1, branches, PIECES)),
+            dma((PIECES,)),
+            dma((PIECES,)),
+            dma((2,)),
         ],
         compiler_params=pltpu.CompilerParams(
             has_side_effects=True, collective_id=0, vmem_limit_bytes=62 * 2**20

time: 105 us -> 101 us (0.962)
  Pallas kernels: 101 us -> 98 us
    pallas_call x1, Pallas kernels: 101 us -> 98 us  [layer(): pl.pallas_call(functools.partial(layer_kernel, n_pre, n_dec), out_shape=(...]
where the time goes in v4:
time: 101 us; the launch traced here: 100 us
  Pallas kernels  98 us (97%)
  local copies, waits for them, and re-layouts  1.77 us (2%)
    pallas_call x1, Pallas kernels, layer(): pl.pallas_call(functools.partial(layer_kernel, n_pre, n_dec), out_shape=(...  98 us

profile of v4, /device:TPU:0, one launch (start us, length us, event | category | flops | bytes accessed | tf_op | source)
XLA Modules:
  0.0 100.4 jit_solution(15026552759159023479)
XLA Ops:
  0.6 98.0 %layer.1 = (bf16[4,128,1024]{2,1,0:T(8,128)(2,1)S(1)}, bf16[4,128,512]{2,1,0:T(8,128)(2,1)S(1)}) custom-call(s32[16,16]{1,0:T(8,128)} %lists_hbm.1, s32[16]{0:T(128)} %reach_hbm.1, s32[16]{0:T(128)} %owner_hbm.1, bf16[4,128,256]{2,1,0:T(8,128)(2,1)} %own_hbm.1, bf16[4,128,256]{2,1,0:T(8,128)(2,1)} %pool_ref.1, bf16[4,128,1024]{2,1,0:T(8,128)(2,1)} %q_hbm.1, ...), custom_call_target="tpu_custom_call" | custom-call | tf_op jit(solution)/shard_map/layer/pallas_call | solution.py:756
  98.6 1.0 copy.11
  99.6 0.8 copy.12

commit v5 on v4

--- a/solution.py
+++ b/solution.py
@@ -365,20 +365,31 @@
         _, src, dst = home_parts(0, part)
         return pltpu.make_async_copy(src, dst, hrecv.at[0, part])
 
+    def homeward(near):
+        for part in range(ratio):
+            for k in range(n_pre):
+                source = lax.rem(pre + k, n_pre) * ratio + part
+                mine = lax.rem(source, 2) == side
+
+                @pl.when(mine if near else jnp.logical_not(mine))
+                def _(k=k, part=part):
+                    if k == 0:
+                        home_local(part).start()
+                    else:
+                        to_home(k, part).start()
+
     def pages_to_side():
         for k in range(1, spots):
             to_row(k).wait_recv()
         row_local.wait()
         to_side.start()
         side_local.start()
+        side_local.wait()
+        homeward(True)
 
     def pages_to_home():
         to_side.wait_recv()
-        side_local.wait()
-        for part in range(ratio):
-            home_local(part).start()
-            for k in range(1, n_pre):
-                to_home(k, part).start()
+        homeward(False)
 
     barrier = pltpu.get_barrier_semaphore()
     for k in range(1, n_pre):

time: 101 us -> 101 us (level)
  no operation moved by 1% of the time
where the time goes in v5:
time: 101 us; the launch traced here: 100 us
  Pallas kernels  97.9 us (97%)
  local copies, waits for them, and re-layouts  1.77 us (2%)
    pallas_call x1, Pallas kernels, layer(): pl.pallas_call(functools.partial(layer_kernel, n_pre, n_dec), out_shape=(...  97.9 us

profile of v5, /device:TPU:0, one launch (start us, length us, event | category | flops | bytes accessed | tf_op | source)
XLA Modules:
  0.0 100.3 jit_solution(3723440071592181385)
XLA Ops:
  0.6 97.9 %layer.1 = (bf16[4,128,1024]{2,1,0:T(8,128)(2,1)S(1)}, bf16[4,128,512]{2,1,0:T(8,128)(2,1)S(1)}) custom-call(s32[16,16]{1,0:T(8,128)} %lists_hbm.1, s32[16]{0:T(128)} %reach_hbm.1, s32[16]{0:T(128)} %owner_hbm.1, bf16[4,128,256]{2,1,0:T(8,128)(2,1)} %own_hbm.1, bf16[4,128,256]{2,1,0:T(8,128)(2,1)} %pool_ref.1, bf16[4,128,1024]{2,1,0:T(8,128)(2,1)} %q_hbm.1, ...), custom_call_target="tpu_custom_call" | custom-call | tf_op jit(solution)/shard_map/layer/pallas_call | solution.py:767
  98.6 1.0 copy.11
  99.5 0.8 copy.12
